TPU v7x, 512 devices: a whole 4x4x16 slice. The times are simulated.
512 devices in a mesh: group: 8 (over z_lo), shard: 64 (over z_hi, x, y, core).
Axes of the slice: x: 4, y: 4, z: 16 (z_hi: 2, z_lo: 8; z = z_hi * 8 + z_lo), core: 2. Of those that a mesh axis runs over, the one named last changes fastest.
Arguments:
- inner_embed: float32 [8, 15360, 768], P('group', 'shard'), may hold values from -6 to 6
- outer_embed: float32 [15360, 768], P('shard'), may hold values from -6 to 6
- moment_embed: float32 [15360, 768], P('shard'), may hold values from -6 to 6
- basis: float32 [15360, 64], P('shard'), may hold values from -6 to 6
- inner_attn: float32 [8, 768, 3072], P('group', 'shard'), may hold values from -6 to 6
- outer_attn: float32 [768, 3072], P(None, 'shard'), may hold values from -6 to 6
- moment_attn: float32 [768, 3072], P(None, 'shard'), may hold values from -6 to 6
- inner_norms: float32 [8, 4, 768], P('group', None, 'shard'), may hold values from -6 to 6
- outer_norms: float32 [4, 768], P(None, 'shard'), may hold values from -6 to 6
- moment_norms: float32 [4, 768], P(None, 'shard'), may hold values from -6 to 6
Outputs:
- new_embed: float32 [15360, 768], P('shard')
- new_moment_embed: float32 [15360, 768], P('shard')
- new_attn: float32 [768, 3072], P(None, 'shard')
- new_moment_attn: float32 [768, 3072], P(None, 'shard')
- new_norms: float32 [4, 768], P(None, 'shard')
- new_moment_norms: float32 [4, 768], P(None, 'shard')
- replica_attn: bfloat16 [768, 3072], P('shard')
All inputs are finite; a program needn't handle non-finite values.
Results may differ from a plain program's by a relative error of at most 0.0004.
Values may be sent and summed in bfloat16 or wider, within the bound.
A program may use at most 64 MiB of HBM per device.

v0:
```python
import math
import jax
import jax.numpy as jnp
from jax import lax
from jax.sharding import PartitionSpec as P

VOCAB = 15360
RANK = 64


def nesterov(outer, moment, delta):
    moment_new = 0.5 * moment + delta
    return (outer - (delta + 0.5 * moment_new), moment_new)


def on_device(
    inner_embed,
    outer_embed,
    moment_embed,
    basis,
    inner_attn,
    outer_attn,
    moment_attn,
    inner_norms,
    outer_norms,
    moment_norms,
):
    groups = lax.axis_size("group")
    embed_diff = outer_embed - inner_embed[0]
    partial_coeff = lax.dot_general(
        basis,
        embed_diff,
        (((0,), (0,)), ((), ())),
        precision=lax.Precision.HIGHEST,
        preferred_element_type=jnp.float32,
    )
    norm_diff = outer_norms - inner_norms[0]
    moved = lax.all_to_all(inner_attn[0], "shard", split_axis=1, concat_axis=0, tiled=True)
    attn_term = outer_attn - moved
    coeff_sum = lax.psum(partial_coeff, ("group", "shard"))
    attn_sum, norm_sum = lax.psum((attn_term, norm_diff), "group")
    attn_delta = attn_sum / groups
    norm_delta = norm_sum / groups
    coefficient = coeff_sum / groups
    embed_delta = jnp.dot(
        basis, coefficient, precision=lax.Precision.HIGHEST, preferred_element_type=jnp.float32
    ) * (1.0 / math.sqrt(RANK * VOCAB))
    new_embed, new_moment_embed = nesterov(outer_embed, moment_embed, embed_delta)
    new_attn, new_moment_attn = nesterov(outer_attn, moment_attn, attn_delta)
    new_norms, new_moment_norms = nesterov(outer_norms, moment_norms, norm_delta)
    replica_attn = lax.all_to_all(
        new_attn.astype(jnp.bfloat16), "shard", split_axis=0, concat_axis=1, tiled=True
    )
    return (
        new_embed,
        new_moment_embed,
        new_attn,
        new_moment_attn,
        new_norms,
        new_moment_norms,
        replica_attn,
    )


def solution(mesh):
    placed = (
        P("group", "shard", None),
        P("shard", None),
        P("shard", None),
        P("shard", None),
        P("group", "shard", None),
        P(None, "shard"),
        P(None, "shard"),
        P("group", None, "shard"),
        P(None, "shard"),
        P(None, "shard"),
    )
    return jax.shard_map(
        on_device,
        mesh=mesh,
        in_specs=placed,
        out_specs=(
            P("shard", None),
            P("shard", None),
            P(None, "shard"),
            P(None, "shard"),
            P(None, "shard"),
            P(None, "shard"),
            P("shard", None),
        ),
        check_vma=False,
    )
```

profile of v0, /device:TPU:1, one launch (start us, length us, event | category | flops | bytes accessed | tf_op | source)
XLA Modules:
  0.0 638.4 jit_solution(14730503204910227283)
XLA Ops:
  7.2 0.0 copy-start
  7.2 1.3 reduce
  8.5 0.2 all_to_all.28
  8.7 0.2 copy.34
  8.9 1.0 reshape.22
  9.9 0.0 copy-start.4
  9.9 22.4 %all-to-all-start = ((f32[64,1,576]{2,1,0:T(1,128)}), f32[64,1,576]{2,1,0:T(1,128)S(1)}, u32[]{:S(2)}, u32[]{:S(2)}) async-start(f32[64,1,576]{2,1,0:T(1,128)} %reshape.22), calls=%async_computation | async-start | bytes 327680 | tf_op jit(solution)/shard_map/all_to_all | solution.py:38
  32.3 0.0 all-reduce.5.cloned.1.call-start
  32.4 0.0 copy-done.4
  32.4 0.2 copy.29
  32.6 17.3 %all-to-all-done = f32[64,1,576]{2,1,0:T(1,128)S(1)} async-done(((f32[64,1,576]{2,1,0:T(1,128)}), f32[64,1,576]{2,1,0:T(1,128)S(1)}, u32[]{:S(2)}, u32[]{:S(2)}) %all-to-all-start) | async-done | bytes 147488 | tf_op jit(solution)/shard_map/all_to_all | solution.py:38
  49.9 0.5 broadcast.29
  50.4 1.0 reduce.1
  51.4 0.2 reshape.23
  51.7 0.0 copy-start.1
  51.7 0.0 copy-start.2
  51.7 0.8 sub.20
  52.5 0.0 all-reduce.5.cloned.1.call-update
  52.5 0.0 all-reduce.3.cloned.1.call-start
  52.6 0.0 copy-done
  52.6 0.4 copy-done.1
  53.0 0.2 copy-done.2
  53.2 1.3 convolution_bitcast_fusion
  54.5 0.0 copy-start.5
  54.5 0.0 all-reduce.3.cloned.1.call-update
  54.5 0.9 copy-done.5
  55.4 0.0 copy-start.6
  55.4 0.0 copy-start.7
  55.4 0.2 copy.28
  55.5 0.5 copy-done.6
  56.1 0.0 copy-done.7
  56.1 0.0 copy-start.8
  56.1 27.7 %psum.23 = f32[4,12]{1,0:T(4,128)S(1)} all-reduce(f32[4,12]{1,0:T(4,128)S(1)} %bitcast_subtract_fusion.2), channel_id=1, replica_groups=mesh['group'=8,'shard'=64] {'group'}, use_global_device_ids=true, to_apply=%region_2.0 | all-reduce | flops 48 | bytes 384 | tf_op jit(solution)/shard_map/psum | solution.py:41
  83.8 0.0 copy-done.8
  83.8 0.6 add_subtract_fusion.2
  84.4 80.6 %all-reduce.5.cloned.1.call-done = f32[768,48]{1,0:T(8,128)} async-done(((f32[768,48]{1,0:T(8,128)}), f32[768,48]{1,0:T(8,128)}) %all-reduce.5.cloned.1.call-update) | async-done | bytes 147472 | tf_op jit(solution)/shard_map/psum | solution.py:41
  165.0 1.1 fusion.4
  166.1 0.0 copy-start.3
  166.1 0.1 all_to_all.32
  166.2 0.9 reshape.24
  167.1 16.1 %all-to-all-start.1 = ((bf16[64,2,288]{2,1,0:T(2,128)(2,1)}), bf16[64,2,288]{2,1,0:T(2,128)(2,1)S(1)}, u32[]{:S(2)}, u32[]{:S(2)}) async-start(bf16[64,2,288]{2,1,0:T(2,128)(2,1)} %reshape.24), calls=%async_computation.1 | async-start | bytes 196608 | tf_op jit(solution)/shard_map/all_to_all | solution.py:51
  183.3 442.5 %all-reduce.3.cloned.1.call-done = f32[64,768]{1,0:T(8,128)} async-done(((f32[64,768]{1,0:T(8,128)}), f32[64,768]{1,0:T(8,128)}) %all-reduce.3.cloned.1.call-update) | async-done | bytes 196624 | tf_op jit(solution)/shard_map/psum | solution.py:40
  625.8 0.0 copy-done.3
  625.8 2.9 add_subtract_fusion
  628.7 0.8 copy.31
  629.5 0.8 copy.32
  630.3 0.0 all-to-all-done.1
  630.3 0.2 reshape.25
  630.6 0.1 copy.30
  630.6 0.9 all_to_all.35
  (3 shorter events, 0.1 us)
Async XLA Ops:
  7.2 45.4 %copy-start = (f32[240,64]{0,1:T(8,128)S(1)}, f32[240,64]{0,1:T(8,128)}, u32[]{:S(2)}) copy-start(f32[240,64]{0,1:T(8,128)} %param.13) | copy-start | bytes 184324
  9.9 22.4 %copy-start.4 = (f32[768,48]{0,1:T(8,128)S(1)}, f32[768,48]{0,1:T(8,128)}, u32[]{:S(2)}) copy-start(f32[768,48]{0,1:T(8,128)} %param.15) | copy-start | bytes 442372
  9.9 39.9 %all-to-all-start = ((f32[64,1,576]{2,1,0:T(1,128)}), f32[64,1,576]{2,1,0:T(1,128)S(1)}, u32[]{:S(2)}, u32[]{:S(2)}) async-start(f32[64,1,576]{2,1,0:T(1,128)} %reshape.22), calls=%async_computation | async-start | bytes 327680 | tf_op jit(solution)/shard_map/all_to_all | solution.py:38
  32.3 132.7 %all-reduce.5.cloned.1.call-start = ((), (), s32[]{:S(2)}) async-start(), calls=%async_computation.3 | async-start | bytes 786432 | tf_op jit(solution)/shard_map/psum | solution.py:41
  51.7 1.3 copy-start.1
  51.7 1.5 copy-start.2
  52.5 573.3 %all-reduce.3.cloned.1.call-start = ((), (), s32[]{:S(2)}) async-start(), calls=%async_computation.2 | async-start | bytes 393216 | tf_op jit(solution)/shard_map/psum | solution.py:40
  54.5 0.9 copy-start.5
  55.4 0.7 copy-start.6
  55.4 0.7 copy-start.7
  56.1 27.7 %copy-start.8 = (f32[4,12]{1,0:T(4,128)S(1)}, f32[4,12]{1,0:T(4,128)}, u32[]{:S(2)}) copy-start(f32[4,12]{1,0:T(4,128)} %param.19) | copy-start | bytes 580
  166.1 459.7 %copy-start.3 = (f32[240,768]{1,0:T(8,128)S(1)}, f32[240,768]{1,0:T(8,128)}, u32[]{:S(2)}) copy-start(f32[240,768]{1,0:T(8,128)} %param.12) | copy-start | bytes 2211844
  167.1 463.2 %all-to-all-start.1 = ((bf16[64,2,288]{2,1,0:T(2,128)(2,1)}), bf16[64,2,288]{2,1,0:T(2,128)(2,1)S(1)}, u32[]{:S(2)}, u32[]{:S(2)}) async-start(bf16[64,2,288]{2,1,0:T(2,128)(2,1)} %reshape.24), calls=%async_computation.1 | async-start | bytes 196608 | tf_op jit(solution)/shard_map/all_to_all | solution.py:51
Sparse Core Ops, SparseCore 0:
  52.7 112.3 all-reduce.4
  171.9 453.8 all-reduce.2
where the time goes:
time: 639 us; the launch traced here: 638 us
  waiting for transfers between devices  540 us (85%)
  starting transfers between devices  38.6 us (6%)
  blocking collectives  27.7 us (4%)
  between operations  14.2 us (2%)
  local copies, waits for them, and re-layouts  8.4 us (1%)
    psum x1, waiting for transfers between devices, on_device(): coeff_sum = lax.psum(partial_coeff, ('group', 'shard'))  442 us
    psum x1, waiting for transfers between devices, on_device(): attn_sum, norm_sum = lax.psum((attn_term, norm_diff), 'group')  80.6 us
    psum x1, blocking collectives, on_device(): attn_sum, norm_sum = lax.psum((attn_term, norm_diff), 'group')  27.7 us
    all_to_all x1, starting transfers between devices, on_device(): lax.all_to_all(inner_attn[0], 'shard', split_axis=1, concat_axis=0, tiled...  22.4 us
    all_to_all x1, waiting for transfers between devices, on_device(): lax.all_to_all(inner_attn[0], 'shard', split_axis=1, concat_axis=0, tiled...  17.3 us
    all_to_all x1, starting transfers between devices, on_device(): lax.all_to_all(new_attn.astype(jnp.bfloat16), 'shard', split_axis=0, conc...  16.1 us
  transfers between devices with their start and end apart: 4, of which 3 were waited for; matrix products, arithmetic and copies ran while one was open for 1% of the time, Pallas kernels for 0%

commit v1 on v0

--- a/solution.py
+++ b/solution.py
@@ -37,7 +37,7 @@
     norm_diff = outer_norms - inner_norms[0]
     moved = lax.all_to_all(inner_attn[0], "shard", split_axis=1, concat_axis=0, tiled=True)
     attn_term = outer_attn - moved
-    coeff_sum = lax.psum(partial_coeff, ("group", "shard"))
+    coeff_sum = lax.psum(lax.psum(partial_coeff, "shard"), "group")
     attn_sum, norm_sum = lax.psum((attn_term, norm_diff), "group")
     attn_delta = attn_sum / groups
     norm_delta = norm_sum / groups

time: 639 us -> 1220 us (1.91)
  waiting for transfers between devices: 540 us -> 1130 us
    psum x2, waiting for transfers between devices: 523 us -> 1100 us  [on_device(): coeff_sum = lax.psum(lax.psum(partial_coeff, 'shard'), 'group')]
    all_to_all x1, waiting for transfers between devices: 0.01 us -> 13.2 us  [on_device(): lax.all_to_all(new_attn.astype(jnp.bfloat16), 'shard', split_axis=0, conc...]
  transfers between devices with their start and end apart: 4 -> 4, of which waited for: 3 -> 4; matrix products, arithmetic and copies ran while one was open for 1% -> 1% of each run, Pallas kernels for 0% -> 0%
where the time goes in v1:
time: 1220 us
  waiting for transfers between devices  1130 us (93%)
  starting transfers between devices  38.2 us (3%)
  blocking collectives  22.7 us (2%)
  between operations  14.2 us (1%)
    psum x2, waiting for transfers between devices, on_device(): coeff_sum = lax.psum(lax.psum(partial_coeff, 'shard'), 'group')  1100 us
  transfers between devices with their start and end apart: 4, of which 4 were waited for; matrix products, arithmetic and copies ran while one was open for 1% of the time, Pallas kernels for 0%

profile of v1, /device:TPU:1, one launch (start us, length us, event | category | flops | bytes accessed | tf_op | source)
XLA Modules:
  0.0 1221.4 jit_solution(6836148899837605894)
XLA Ops:
  7.2 0.0 copy-start
  7.2 1.3 reduce
  8.5 0.2 all_to_all.28
  8.7 0.0 copy-start.2
  8.7 0.2 copy.34
  8.9 0.0 copy-start.1
  8.9 1.0 reshape.22
  10.0 22.2 %all-to-all-start = ((f32[64,1,576]{2,1,0:T(1,128)}), f32[64,1,576]{2,1,0:T(1,128)S(1)}, u32[]{:S(2)}, u32[]{:S(2)}) async-start(f32[64,1,576]{2,1,0:T(1,128)} %reshape.22), calls=%async_computation | async-start | bytes 327680 | tf_op jit(solution)/shard_map/all_to_all | solution.py:38
  32.2 0.0 all-reduce.4.cloned.1.call-start
  32.3 0.0 copy-done
  32.3 0.0 copy-done.2
  32.3 0.0 copy-done.1
  32.3 1.3 convolution_bitcast_fusion
  33.6 0.0 copy-start.5
  33.6 0.0 all-reduce.4.cloned.1.call-update
  33.6 0.0 copy-start.6
  33.6 0.0 all-reduce.6.cloned.1.call-start
  33.7 0.8 copy-done.5
  34.5 0.2 copy.29
  34.7 0.0 copy-done.6
  34.7 0.2 copy.28
  34.8 14.9 %all-to-all-done = f32[64,1,576]{2,1,0:T(1,128)S(1)} async-done(((f32[64,1,576]{2,1,0:T(1,128)}), f32[64,1,576]{2,1,0:T(1,128)S(1)}, u32[]{:S(2)}, u32[]{:S(2)}) %all-to-all-start) | async-done | bytes 147488 | tf_op jit(solution)/shard_map/all_to_all | solution.py:38
  49.7 0.5 broadcast.29
  50.3 1.0 reduce.1
  51.3 0.2 reshape.23
  51.6 0.8 sub.20
  52.4 1004.4 %all-reduce.4.cloned.1.call-done = f32[64,768]{1,0:T(8,128)} async-done(((f32[64,768]{1,0:T(8,128)}), f32[64,768]{1,0:T(8,128)}) %all-reduce.4.cloned.1.call-update) | async-done | bytes 196624 | tf_op jit(solution)/shard_map/psum | solution.py:40
  1056.8 0.0 copy-start.7
  1056.8 0.0 copy-start.8
  1056.8 0.0 all-reduce.6.cloned.1.call-update
  1056.8 0.7 copy-done.7
  1057.5 0.0 copy-done.8
  1057.5 0.0 copy-start.9
  1057.5 22.7 %psum.31 = f32[4,12]{1,0:T(4,128)S(1)} all-reduce(f32[4,12]{1,0:T(4,128)S(1)} %bitcast_subtract_fusion.2), channel_id=1, replica_groups=mesh['group'=8,'shard'=64] {'group'}, use_global_device_ids=true, to_apply=%region_3.0 | all-reduce | flops 48 | bytes 384 | tf_op jit(solution)/shard_map/psum | solution.py:41
  1080.2 0.0 copy-done.9
  1080.2 0.6 add_subtract_fusion.2
  1080.8 97.6 %all-reduce.6.cloned.1.call-done = (f32[64,768]{1,0:T(8,128)}, f32[768,48]{1,0:T(8,128)}) async-done(((f32[64,768]{1,0:T(8,128)}, f32[768,48]{1,0:T(8,128)}), (f32[64,768]{1,0:T(8,128)}, f32[768,48]{1,0:T(8,128)})) %all-reduce.6.cloned.1.call-update) | async-done | bytes 344080 | tf_op jit(solution)/shard_map/psum | solution.py:40
  1178.4 1.1 fusion.4
  1179.5 0.1 all_to_all.32
  1179.6 0.0 copy-start.3
  1179.6 0.9 reshape.24
  1180.5 15.8 %all-to-all-start.1 = ((bf16[64,2,288]{2,1,0:T(2,128)(2,1)}), bf16[64,2,288]{2,1,0:T(2,128)(2,1)S(1)}, u32[]{:S(2)}, u32[]{:S(2)}) async-start(bf16[64,2,288]{2,1,0:T(2,128)(2,1)} %reshape.24), calls=%async_computation.1 | async-start | bytes 196608 | tf_op jit(solution)/shard_map/all_to_all | solution.py:51
  1196.4 0.8 copy.31
  1197.2 0.0 copy-start.4
  1197.2 0.8 copy.32
  1198.0 0.0 copy-done.3
  1198.0 0.1 copy-done.4
  1198.1 2.0 add_subtract_fusion
  1200.1 13.2 %all-to-all-done.1 = bf16[64,2,288]{2,1,0:T(2,128)(2,1)S(1)} async-done(((bf16[64,2,288]{2,1,0:T(2,128)(2,1)}), bf16[64,2,288]{2,1,0:T(2,128)(2,1)S(1)}, u32[]{:S(2)}, u32[]{:S(2)}) %all-to-all-start.1) | async-done | bytes 73760 | tf_op jit(solution)/shard_map/all_to_all | solution.py:51
  1213.3 0.2 reshape.25
  1213.6 0.1 copy.30
  1213.6 0.9 all_to_all.35
  (3 shorter events, 0.1 us)
Async XLA Ops:
  7.2 25.1 %copy-start = (f32[240,64]{0,1:T(8,128)S(1)}, f32[240,64]{0,1:T(8,128)}, u32[]{:S(2)}) copy-start(f32[240,64]{0,1:T(8,128)} %param.13) | copy-start | bytes 184324
  8.7 23.6 %copy-start.2 = (f32[1,240,768]{2,1,0:T(8,128)S(1)}, f32[1,240,768]{2,1,0:T(8,128)}, u32[]{:S(2)}) copy-start(f32[1,240,768]{2,1,0:T(8,128)} %param.10) | copy-start | bytes 2211844
  8.9 23.4 %copy-start.1 = (f32[240,768]{1,0:T(8,128)S(1)}, f32[240,768]{1,0:T(8,128)}, u32[]{:S(2)}) copy-start(f32[240,768]{1,0:T(8,128)} %param.11) | copy-start | bytes 2211844
  10.0 39.8 %all-to-all-start = ((f32[64,1,576]{2,1,0:T(1,128)}), f32[64,1,576]{2,1,0:T(1,128)S(1)}, u32[]{:S(2)}, u32[]{:S(2)}) async-start(f32[64,1,576]{2,1,0:T(1,128)} %reshape.22), calls=%async_computation | async-start | bytes 327680 | tf_op jit(solution)/shard_map/all_to_all | solution.py:38
  32.2 1024.6 %all-reduce.4.cloned.1.call-start = ((), (), s32[]{:S(2)}) async-start(), calls=%async_computation.2 | async-start | bytes 393216 | tf_op jit(solution)/shard_map/psum | solution.py:40
  33.6 0.9 copy-start.5
  33.6 1.1 copy-start.6
  33.6 1144.8 %all-reduce.6.cloned.1.call-start = ((), (), s32[]{:S(2)}) async-start(), calls=%async_computation.3 | async-start | bytes 1179648 | tf_op jit(solution)/shard_map/psum | solution.py:40
  1056.8 0.7 copy-start.7
  1056.8 0.7 copy-start.8
  1057.5 22.7 %copy-start.9 = (f32[4,12]{1,0:T(4,128)S(1)}, f32[4,12]{1,0:T(4,128)}, u32[]{:S(2)}) copy-start(f32[4,12]{1,0:T(4,128)} %param.19) | copy-start | bytes 580
  1179.6 18.4 %copy-start.3 = (f32[240,768]{1,0:T(8,128)S(1)}, f32[240,768]{1,0:T(8,128)}, u32[]{:S(2)}) copy-start(f32[240,768]{1,0:T(8,128)} %param.12) | copy-start | bytes 2211844
  1180.5 32.8 %all-to-all-start.1 = ((bf16[64,2,288]{2,1,0:T(2,128)(2,1)}), bf16[64,2,288]{2,1,0:T(2,128)(2,1)S(1)}, u32[]{:S(2)}, u32[]{:S(2)}) async-start(bf16[64,2,288]{2,1,0:T(2,128)(2,1)} %reshape.24), calls=%async_computation.1 | async-start | bytes 196608 | tf_op jit(solution)/shard_map/all_to_all | solution.py:51
  1197.2 0.9 copy-start.4
Sparse Core Ops, SparseCore 0:
  36.5 1020.1 all-reduce.3
  1060.6 117.7 all-reduce.5
